TPU v7x, 32 devices: a whole 2x2x4 slice. The times are simulated.
32 devices in a mesh: band: 8 (over y, x, core), pair: 4 (over z).
Axes of the slice: x: 2, y: 2, z: 4, core: 2. Of those that a mesh axis runs over, the one named last changes fastest.
Arguments:
- orbitals: bfloat16 [16, 32, 1024], P('band'), may hold values from -6 to 6
- kernel: float32 [32, 1024], replicated, may hold values from 0 to 1.2, as said below
- occupations: float32 [16], replicated, may hold values from 0.04 to 0.99
- plan: int32 [8], replicated, may hold values from 0 to 7, each once
Outputs:
- exchange: float32 [16, 32, 1024], P('band', 'pair')
- slot_energy: float32 [8], P('pair')
Inputs may be any that keep to these rules, and one draw needn't show every extreme that they name: `plan`: each owner distance 0 to 7 appears exactly once. kernel is unchanged when any one frequency index i is replaced by (32 - i) % 32, and is not negative.
All inputs are finite; a program needn't handle non-finite values.
Results may differ from a plain program's by a relative error of at most 0.0004.
Values may be sent and summed in bfloat16 or wider, within the bound.
A program may use at most 64 MiB of HBM per device.

v0:
```python
import functools
import math

import jax
import jax.numpy as jnp
import ml_dtypes
import numpy as np
from jax import lax
from jax.experimental import pallas as pl
from jax.experimental.pallas import tpu as pltpu
from jax.sharding import PartitionSpec as P

MESH = pl.DeviceIdType.MESH
F32 = jnp.float32
BF16 = jnp.bfloat16


def pieces(value, count):
    terms = []
    for at in range(count):
        term = value.astype(BF16)
        terms.append(term)
        if at < count - 1:
            value = value - term.astype(F32)
    return terms


def tables(points):
    half = points // 2
    block = half * half
    sw, row, col = (x.reshape(-1) for x in np.meshgrid(np.arange(2), np.arange(half), np.arange(half), indexing="ij"))
    target = np.arange(2 * block)
    place = np.where(sw == 0, col, points - 1 - col)
    fold = np.zeros((2, 2 * block, 2 * block), np.float32)
    fold[0, row * points + place, target] = 1.0
    fold[1, (half - 1 - row) * points + place, target] = 1.0
    select = np.zeros((2 * block, 2 * block), np.float32)
    select[row * points + col + sw, target] = 1.0
    spot = np.arange(half) + 0.5
    basis = []
    for odd in range(2):
        mode = np.arange(half) + odd
        angle = 2.0 * np.pi * mode[:, None] * spot[None, :] / points
        edge = (mode == 0) | (mode == half)
        factor = np.where(edge, math.sqrt(1.0 / half), math.sqrt(2.0 / half))
        basis.append((np.sin(angle) if odd else np.cos(angle)) * factor[:, None])
    joint = np.stack([np.kron(basis[v], basis[w]).T for v in range(2) for w in range(2)])
    high = joint.astype(ml_dtypes.bfloat16)
    low = (joint - high.astype(np.float64)).astype(ml_dtypes.bfloat16)
    shift = np.arange(-(-(half + 1) // 8) * 8)
    cosine = np.cos(2.0 * np.pi * shift[:, None] * np.arange(points)[None, :] / points) / (4.0 * points)
    maps = np.concatenate([fold, select[None]]).astype(ml_dtypes.bfloat16)
    return maps, np.stack([high, low]), cosine.astype(np.float32)


def kernel(
    dims,
    plan_ref, occ_ref, orb_ref, ker_ref, cos_ref, maps_hbm, joint_hbm,
    out_ref, slot_ref,
    held, maps, joint, left, right, spread, lhs, spectrum, field, total, tile, sums, band_in, pair_in,
    load_sem, send_sem, recv_sem, band_send, band_recv, pair_send, pair_recv,
):
    n_band, n_pair, points, per_owner = dims
    meets = n_band // n_pair
    plane = points * points
    half = points // 2
    block = half * half
    planes = points // n_pair
    pairs = per_owner * per_owner * meets
    rows = points * pairs
    me = lax.axis_index("band")
    group = lax.axis_index("pair")
    base = group * planes

    loads = [
        pltpu.make_async_copy(maps_hbm, maps, load_sem.at[0]),
        pltpu.make_async_copy(joint_hbm, joint, load_sem.at[1]),
    ]
    for load in loads:
        load.start()

    barrier = pltpu.get_barrier_semaphore()
    for x in range(1, n_band):
        pl.semaphore_signal(barrier, inc=1, device_id={"band": me ^ x}, device_id_type=MESH)
    for x in range(1, n_pair):
        pl.semaphore_signal(barrier, inc=1, device_id={"pair": group ^ x}, device_id_type=MESH)
    pl.semaphore_wait(barrier, n_band + n_pair - 2)

    def order(step):
        first = jnp.maximum(group, 1) - 1
        return jnp.where(step == 0, 0, 1 + lax.rem(first + step - 1 + (n_pair - 1), n_pair - 1))

    def move(src, chunk, member, target):
        return pltpu.make_async_remote_copy(
            src_ref=src,
            dst_ref=held.at[chunk, member],
            send_sem=send_sem.at[chunk, member],
            recv_sem=recv_sem.at[chunk, member],
            device_id={"band": target},
            device_id_type=MESH,
        )

    for m in range(1, meets):
        move(orb_ref, 0, m, me ^ m).start()

    def send_direct(step, carry):
        chunk = order(step)
        move(orb_ref, chunk, 0, me ^ (chunk * meets)).start()
        return carry

    lax.fori_loop(1, n_pair, send_direct, 0)

    held[0, 0] = orb_ref[...]
    total[...] = jnp.zeros_like(total)

    mixed = jnp.dot(cos_ref[...], ker_ref[...], precision=lax.Precision.HIGHEST, preferred_element_type=F32)
    shifted = pltpu.roll(mixed, plane - points, 1)
    loads[0].wait()
    for v, source in enumerate((mixed, shifted)):
        picked = 0.0
        for term in pieces(source[:, : 2 * block], 3):
            picked = picked + jnp.dot(term, maps[2], preferred_element_type=F32)
        for s in range(half + 1):
            spread[s, :, v * 2 * block : (v + 1) * 2 * block] = jnp.broadcast_to(
                picked[s : s + 1], (8, 2 * block)
            )

    def folded(raw):
        return [
            jnp.dot(raw[:, v * 2 * block : (v + 1) * 2 * block], maps[v], preferred_element_type=F32)
            for v in range(2)
        ]

    own = folded(orb_ref[...].reshape(per_owner * points, plane))
    per_a = meets * per_owner
    for a in range(per_owner):
        for v in range(2):
            value = own[v][a * points : (a + 1) * points]
            for o in range(per_a):
                left[:, a * per_a + o, v * 2 * block : (v + 1) * 2 * block] = value
    loads[1].wait()

    sub = lax.broadcasted_iota(jnp.int32, (pairs, 128), 0)

    def convolve(start, t):
        lanes = slice(t * 128, (t + 1) * 128)
        y = [spectrum[lax.rem(start + i, points), :, lanes] for i in range(points)]
        z = []
        for j in range(planes):
            value = spread[0, :, lanes] * y[j] + spread[half, :, lanes] * y[(j + half) % points]
            for s in range(1, half):
                value = value + spread[s, :, lanes] * (y[(j + s) % points] + y[(j - s) % points])
            z.append(value)
        return y, z

    def step_body(step, carry):
        chunk = order(step)

        @pl.when(step == 2)
        def _():
            for x in range(1, n_band):
                pltpu.make_async_remote_copy(
                    src_ref=tile, dst_ref=band_in.at[x], send_sem=band_send.at[x], recv_sem=band_recv.at[x],
                    device_id={"band": me ^ x}, device_id_type=MESH,
                ).start()

        for m in range(1, meets):
            move(orb_ref, chunk, m, me ^ m).wait_recv()
        moved = folded(held[chunk].reshape(meets * per_owner * points, plane))
        for v in range(2):
            for o in range(per_a):
                value = moved[v][o * points : (o + 1) * points]
                for a in range(per_owner):
                    right[:, a * per_a + o, v * 2 * block : (v + 1) * 2 * block] = value

        density = (left[...] * right[...]).reshape(rows, plane)
        part = [density[:, q * block : (q + 1) * block] for q in range(4)]
        s0, d0 = part[0] + part[1], part[0] - part[1]
        s1, d1 = part[2] + part[3], part[2] - part[3]
        for q, value in enumerate((s0 + s1, d0 + d1, s0 - s1, d0 - d1)):
            high, low = pieces(value, 2)
            lhs[q, :, :block] = high
            lhs[q, :, block:] = low
        for q in range(4):
            high, low = lhs[q, :, :block], lhs[q, :, block:]
            modes = jnp.dot(high, joint[0, q], preferred_element_type=F32)
            modes = modes + jnp.dot(low, joint[0, q], preferred_element_type=F32)
            modes = modes + jnp.dot(high, joint[1, q], preferred_element_type=F32)
            spectrum[:, :, q * block : (q + 1) * block] = modes.reshape(points, pairs, block)

        @pl.when(step < n_pair - 1)
        def _():
            later = order(step + 1)
            move(orb_ref, later, 0, me ^ (later * meets)).wait_recv()
            for m in range(1, meets):
                move(held.at[later, 0], later, m, me ^ m).start()

        @pl.when(step == 3)
        def _():
            for x in range(1, n_pair):
                pltpu.make_async_remote_copy(
                    src_ref=sums, dst_ref=pair_in.at[x], send_sem=pair_send.at[x], recv_sem=pair_recv.at[x],
                    device_id={"pair": group ^ x}, device_id_type=MESH,
                ).start()

        for t in range(plane // 128):
            y, z = convolve(base, t)
            for j in range(planes):
                field[j, :, t * 128 : (t + 1) * 128] = z[j]

        occ_b = jnp.zeros((pairs, 128), F32)
        occ_a = jnp.zeros((pairs, 128), F32)
        for m in range(meets):
            partner = me ^ (chunk * meets + m)
            for b in range(per_owner):
                weight = occ_ref[partner * per_owner + b]
                occ_b = jnp.where(lax.rem(sub, per_a) == m * per_owner + b, weight, occ_b)
        for a in range(per_owner):
            occ_a = jnp.where(sub // per_a == a, occ_ref[me * per_owner + a], occ_a)

        @pl.when(chunk == group)
        def _():
            def more(h, acc):
                start = lax.rem(base + h * planes, points)
                for t in range(plane // 128):
                    y, z = convolve(start, t)
                    for j in range(planes):
                        acc = acc + y[j] * z[j]
                return acc

            acc = lax.fori_loop(0, n_pair, more, jnp.zeros((pairs, 128), F32))
            tile[...] = acc * occ_a * occ_b

        z = field[...].reshape(planes * pairs, plane)
        back = []
        for q in range(4):
            high, low = pieces(z[:, q * block : (q + 1) * block], 2)
            value = lax.dot_general(high, joint[0, q], (((1,), (1,)), ((), ())), preferred_element_type=F32)
            value = value + lax.dot_general(low, joint[0, q], (((1,), (1,)), ((), ())), preferred_element_type=F32)
            value = value + lax.dot_general(high, joint[1, q], (((1,), (1,)), ((), ())), preferred_element_type=F32)
            back.append(value)
        s0, d0 = back[0] + back[1], back[0] - back[1]
        s1, d1 = back[2] + back[3], back[2] - back[3]
        scale = jnp.concatenate([occ_b] * (block // 128), axis=1)[None]
        for q, value in enumerate((s0 + s1, d0 + d1, s0 - s1, d0 - d1)):
            cut = slice(q * block, (q + 1) * block)
            potential = value.reshape(planes, pairs, block)
            total[:, :, cut] += potential * (right[pl.ds(base, planes), :, cut] * scale)

        @pl.when(step == 2)
        def _():
            acc = tile[...]
            for x in range(1, n_band):
                pltpu.make_async_remote_copy(
                    src_ref=tile, dst_ref=band_in.at[x], send_sem=band_send.at[x], recv_sem=band_recv.at[x],
                    device_id={"band": me ^ x}, device_id_type=MESH,
                ).wait()
                acc = acc + band_in[x]
            sums[...] = acc

        return carry

    lax.fori_loop(0, n_pair, step_body, 0)

    for a in range(per_owner):
        value = total[:, a * per_a, :]
        for o in range(1, per_a):
            value = value + total[:, a * per_a + o, :]
        for v in range(2):
            result = 0.0
            for term in pieces(value[:, v * 2 * block : (v + 1) * 2 * block], 3):
                result = result + lax.dot_general(
                    term, maps[v], (((1,), (1,)), ((), ())), preferred_element_type=F32
                )
            out_ref[a, :, v * 2 * block : (v + 1) * 2 * block] = -result

    for x in range(1, n_pair):
        pltpu.make_async_remote_copy(
            src_ref=sums, dst_ref=pair_in.at[x], send_sem=pair_send.at[x], recv_sem=pair_recv.at[x],
            device_id={"pair": group ^ x}, device_id_type=MESH,
        ).wait()
    member = lax.rem(sub, per_a) // per_owner
    for s in range(meets):
        wanted = plan_ref[group * meets + s]
        acc = jnp.zeros((pairs, 128), F32)
        for x in range(n_pair):
            value = sums[...] if x == 0 else pair_in[x]
            acc = acc + jnp.where((group ^ x) * meets + member == wanted, value, 0.0)
        slot_ref[s] = -jnp.sum(acc) * (1.0 / (2.0 * n_band * per_owner * points**3))

    for m in range(1, meets):
        move(orb_ref, 0, m, me ^ m).wait_send()

    def drain(step, carry):
        chunk = order(step)
        move(orb_ref, chunk, 0, me ^ (chunk * meets)).wait_send()
        for m in range(1, meets):
            move(held.at[chunk, 0], chunk, m, me ^ m).wait_send()
        return carry

    lax.fori_loop(1, n_pair, drain, 0)


def solution(mesh):
    n_band, n_pair = mesh.shape["band"], mesh.shape["pair"]
    meets = n_band // n_pair

    def on_device(orbitals, ker, occupations, plan):
        per_owner, points, plane = orbitals.shape
        planes = points // n_pair
        pairs = per_owner * per_owner * meets
        block = plane // 4
        maps, joint, cosine = tables(points)
        vmem = pl.BlockSpec(memory_space=pltpu.VMEM)
        smem = pl.BlockSpec(memory_space=pltpu.SMEM)
        anyw = pl.BlockSpec(memory_space=pl.ANY)
        dma = pltpu.SemaphoreType.DMA
        return pl.pallas_call(
            functools.partial(kernel, (n_band, n_pair, points, per_owner)),
            out_shape=(
                jax.ShapeDtypeStruct((per_owner, planes, plane), F32),
                jax.ShapeDtypeStruct((meets,), F32),
            ),
            in_specs=[smem, smem, vmem, vmem, vmem, anyw, anyw],
            out_specs=(vmem, smem),
            scratch_shapes=[
                pltpu.VMEM((n_pair, meets, per_owner, points, plane), BF16),
                pltpu.VMEM(maps.shape, BF16),
                pltpu.VMEM(joint.shape, BF16),
                pltpu.VMEM((points, pairs, plane), F32),
                pltpu.VMEM((points, pairs, plane), F32),
                pltpu.VMEM((points // 2 + 1, 8, plane), F32),
                pltpu.VMEM((4, points * pairs, 2 * block), BF16),
                pltpu.VMEM((points, pairs, plane), F32),
                pltpu.VMEM((planes, pairs, plane), F32),
                pltpu.VMEM((planes, pairs, plane), F32),
                pltpu.VMEM((pairs, 128), F32),
                pltpu.VMEM((pairs, 128), F32),
                pltpu.VMEM((n_band, pairs, 128), F32),
                pltpu.VMEM((n_pair, pairs, 128), F32),
                dma((2,)),
                dma((n_pair, meets)),
                dma((n_pair, meets)),
                dma((n_band,)),
                dma((n_band,)),
                dma((n_pair,)),
                dma((n_pair,)),
            ],
            compiler_params=pltpu.CompilerParams(
                collective_id=0, has_side_effects=True, vmem_limit_bytes=48 * 1024 * 1024
            ),
        )(plan, occupations, orbitals, ker, jnp.asarray(cosine), jnp.asarray(maps), jnp.asarray(joint))

    return jax.shard_map(
        on_device,
        mesh=mesh,
        in_specs=(P("band", None, None), P(), P(), P()),
        out_specs=(P("band", "pair", None), P("pair")),
        check_vma=False,
    )
```

profile of v0, /device:TPU:0, one launch (start us, length us, event | category | flops | bytes accessed | tf_op | source)
XLA Modules:
  0.0 36.0 jit_solution(16083835709780054325)
XLA Ops:
  0.6 0.0 copy-start
  0.6 1.4 %copy-done = bf16[3,512,512]{2,1,0:T(8,128)(2,1)S(1)} copy-done((bf16[3,512,512]{2,1,0:T(8,128)(2,1)S(1)}, bf16[3,512,512]{2,1,0:T(8,128)(2,1)}, u32[]{:S(2)}) %copy-start) | copy-done | bytes 1572888
  2.0 0.0 copy-start.1
  2.0 1.2 %copy-done.1 = bf16[2,4,256,256]{3,2,1,0:T(8,128)(2,1)S(1)} copy-done((bf16[2,4,256,256]{3,2,1,0:T(8,128)(2,1)S(1)}, bf16[2,4,256,256]{3,2,1,0:T(8,128)(2,1)}, u32[]{:S(2)}) %copy-start.1) | copy-done | bytes 1048600
  3.3 0.0 copy-start.2
  3.3 0.9 %copy-done.2 = bf16[2,32,1024]{2,1,0:T(8,128)(2,1)S(1)} copy-done((bf16[2,32,1024]{2,1,0:T(8,128)(2,1)S(1)}, bf16[2,32,1024]{2,1,0:T(8,128)(2,1)}, u32[]{:S(2)}) %copy-start.2) | copy-done | bytes 131096
  4.2 0.0 copy-start.3
  4.2 0.9 %copy-done.3 = f32[32,1024]{1,0:T(8,128)S(1)} copy-done((f32[32,1024]{1,0:T(8,128)S(1)}, f32[32,1024]{1,0:T(8,128)}, u32[]{:S(2)}) %copy-start.3) | copy-done | bytes 131096
  5.1 0.0 copy-start.4
  5.1 0.7 %copy-done.4 = f32[24,32]{1,0:T(8,128)S(1)} copy-done((f32[24,32]{1,0:T(8,128)S(1)}, f32[24,32]{1,0:T(8,128)}, u32[]{:S(2)}) %copy-start.4) | copy-done | bytes 3096
  5.8 0.0 copy-start.5
  5.8 0.7 %copy-done.5 = s32[8]{0:T(128)S(1)} copy-done((s32[8]{0:T(128)S(1)}, s32[8]{0:T(128)}, u32[]{:S(2)}) %copy-start.5) | copy-done | bytes 56
  6.4 0.0 copy-start.6
  6.4 0.7 %copy-done.6 = f32[16]{0:T(128)S(1)} copy-done((f32[16]{0:T(128)S(1)}, f32[16]{0:T(128)}, u32[]{:S(2)}) %copy-start.6) | copy-done | bytes 88
  7.1 27.8 %shard_map.86 = (f32[2,8,1024]{2,1,0:T(8,128)S(1)}, f32[2]{0:T(128)S(1)}) custom-call(s32[8]{0:T(128)S(1)} %copy-done.5, f32[16]{0:T(128)S(1)} %copy-done.6, bf16[2,32,1024]{2,1,0:T(8,128)(2,1)S(1)} %copy-done.2, f32[32,1024]{1,0:T(8,128)S(1)} %copy-done.3, f32[24,32]{1,0:T(8,128)S(1)} %copy-done.4, bf16[3,512,512]{2,1,0:T(8,128)(2,1)S(1)} %copy-done, ...), custom_call_target="tpu_custom_call" | custom-call | tf_op jit(solution)/shard_map/pallas_call | solution.py:318
  34.9 0.6 %copy.11 = f32[2,8,1024]{2,1,0:T(8,128)} copy(f32[2,8,1024]{2,1,0:T(8,128)S(1)} %get-tuple-element.4) | data formatting | bytes 131072
  35.5 0.5 %copy.12 = f32[2]{0:T(128)} copy(f32[2]{0:T(128)S(1)} %get-tuple-element.5) | data formatting | bytes 16
Async XLA Ops:
  0.6 1.4 %copy-start = (bf16[3,512,512]{2,1,0:T(8,128)(2,1)S(1)}, bf16[3,512,512]{2,1,0:T(8,128)(2,1)}, u32[]{:S(2)}) copy-start(bf16[3,512,512]{2,1,0:T(8,128)(2,1)} %constant.7.clone.maps_hbm) | copy-start | bytes 4718596
  2.0 1.2 %copy-start.1 = (bf16[2,4,256,256]{3,2,1,0:T(8,128)(2,1)S(1)}, bf16[2,4,256,256]{3,2,1,0:T(8,128)(2,1)}, u32[]{:S(2)}) copy-start(bf16[2,4,256,256]{3,2,1,0:T(8,128)(2,1)} %constant.8.clone.joint_hbm) | copy-start | bytes 3145732
  3.3 0.9 %copy-start.2 = (bf16[2,32,1024]{2,1,0:T(8,128)(2,1)S(1)}, bf16[2,32,1024]{2,1,0:T(8,128)(2,1)}, u32[]{:S(2)}) copy-start(bf16[2,32,1024]{2,1,0:T(8,128)(2,1)} %orb_ref.1) | copy-start | bytes 393220
  4.2 0.9 %copy-start.3 = (f32[32,1024]{1,0:T(8,128)S(1)}, f32[32,1024]{1,0:T(8,128)}, u32[]{:S(2)}) copy-start(f32[32,1024]{1,0:T(8,128)} %ker_ref.1) | copy-start | bytes 393220
  5.1 0.7 %copy-start.4 = (f32[24,32]{1,0:T(8,128)S(1)}, f32[24,32]{1,0:T(8,128)}, u32[]{:S(2)}) copy-start(f32[24,32]{1,0:T(8,128)} %constant.6.clone.cos_ref) | copy-start | bytes 9220
  5.8 0.7 %copy-start.5 = (s32[8]{0:T(128)S(1)}, s32[8]{0:T(128)}, u32[]{:S(2)}) copy-start(s32[8]{0:T(128)} %plan_ref.1) | copy-start | bytes 100
  6.4 0.7 %copy-start.6 = (f32[16]{0:T(128)S(1)}, f32[16]{0:T(128)}, u32[]{:S(2)}) copy-start(f32[16]{0:T(128)} %occ_ref.1) | copy-start | bytes 196
where the time goes:
time: 36.3 us; the launch traced here: 36 us
  Pallas kernels  27.8 us (77%)
  local copies, waits for them, and re-layouts  7.59 us (21%)
  between operations  0.65 us (2%)
    pallas_call x1, Pallas kernels, on_device(): pl.pallas_call(functools.partial(kernel, (n_band, n_pair, points, per_own...  27.8 us
    unnamed x16, local copies, waits for them, and re-layouts  7.59 us

commit v1 on v0

--- a/solution.py
+++ b/solution.py
@@ -55,9 +55,9 @@
 
 def kernel(
     dims,
-    plan_ref, occ_ref, orb_ref, ker_ref, cos_ref, maps_hbm, joint_hbm,
+    plan_hbm, occ_hbm, orb_ref, ker_hbm, cos_hbm, maps_hbm, joint_hbm,
     out_ref, slot_ref,
-    held, maps, joint, left, right, spread, lhs, spectrum, field, total, tile, sums, band_in, pair_in,
+    plan_ref, occ_ref, ker_ref, cos_ref, held, maps, joint, left, right, spread, lhs, spectrum, field, total, tile, sums, band_in, pair_in,
     load_sem, send_sem, recv_sem, band_send, band_recv, pair_send, pair_recv,
 ):
     n_band, n_pair, points, per_owner = dims
@@ -72,10 +72,11 @@
     group = lax.axis_index("pair")
     base = group * planes
 
-    loads = [
-        pltpu.make_async_copy(maps_hbm, maps, load_sem.at[0]),
-        pltpu.make_async_copy(joint_hbm, joint, load_sem.at[1]),
-    ]
+    wanted_loads = (
+        (orb_ref, held.at[0, 0]), (cos_hbm, cos_ref), (ker_hbm, ker_ref), (maps_hbm, maps),
+        (joint_hbm, joint), (plan_hbm, plan_ref), (occ_hbm, occ_ref),
+    )
+    loads = [pltpu.make_async_copy(src, dst, load_sem.at[at]) for at, (src, dst) in enumerate(wanted_loads)]
     for load in loads:
         load.start()
 
@@ -110,12 +111,13 @@
 
     lax.fori_loop(1, n_pair, send_direct, 0)
 
-    held[0, 0] = orb_ref[...]
     total[...] = jnp.zeros_like(total)
 
+    loads[1].wait()
+    loads[2].wait()
     mixed = jnp.dot(cos_ref[...], ker_ref[...], precision=lax.Precision.HIGHEST, preferred_element_type=F32)
     shifted = pltpu.roll(mixed, plane - points, 1)
-    loads[0].wait()
+    loads[3].wait()
     for v, source in enumerate((mixed, shifted)):
         picked = 0.0
         for term in pieces(source[:, : 2 * block], 3):
@@ -131,14 +133,16 @@
             for v in range(2)
         ]
 
-    own = folded(orb_ref[...].reshape(per_owner * points, plane))
+    loads[0].wait()
+    own = folded(held[0, 0].reshape(per_owner * points, plane))
     per_a = meets * per_owner
     for a in range(per_owner):
         for v in range(2):
             value = own[v][a * points : (a + 1) * points]
             for o in range(per_a):
                 left[:, a * per_a + o, v * 2 * block : (v + 1) * 2 * block] = value
-    loads[1].wait()
+    for load in loads[4:]:
+        load.wait()
 
     sub = lax.broadcasted_iota(jnp.int32, (pairs, 128), 0)
 
@@ -321,9 +325,13 @@
                 jax.ShapeDtypeStruct((per_owner, planes, plane), F32),
                 jax.ShapeDtypeStruct((meets,), F32),
             ),
-            in_specs=[smem, smem, vmem, vmem, vmem, anyw, anyw],
+            in_specs=[anyw] * 7,
             out_specs=(vmem, smem),
             scratch_shapes=[
+                pltpu.SMEM(plan.shape, jnp.int32),
+                pltpu.SMEM(occupations.shape, F32),
+                pltpu.VMEM(ker.shape, F32),
+                pltpu.VMEM(cosine.shape, F32),
                 pltpu.VMEM((n_pair, meets, per_owner, points, plane), BF16),
                 pltpu.VMEM(maps.shape, BF16),
                 pltpu.VMEM(joint.shape, BF16),
@@ -338,7 +346,7 @@
                 pltpu.VMEM((pairs, 128), F32),
                 pltpu.VMEM((n_band, pairs, 128), F32),
                 pltpu.VMEM((n_pair, pairs, 128), F32),
-                dma((2,)),
+                dma((7,)),
                 dma((n_pair, meets)),
                 dma((n_pair, meets)),
                 dma((n_band,)),
@@ -347,7 +355,7 @@
                 dma((n_pair,)),
             ],
             compiler_params=pltpu.CompilerParams(
-                collective_id=0, has_side_effects=True, vmem_limit_bytes=48 * 1024 * 1024
+                collective_id=0, has_side_effects=True, vmem_limit_bytes=67043328
             ),
         )(plan, occupations, orbitals, ker, jnp.asarray(cosine), jnp.asarray(maps), jnp.asarray(joint))
 

time: 36.3 us -> 30.8 us (0.85)
  local copies, waits for them, and re-layouts: 7.59 us -> 2.59 us
  Pallas kernels: 27.8 us -> 27.4 us
    unnamed x16 -> x2, local copies, waits for them, and re-layouts: 7.59 us -> 2.59 us
where the time goes in v1:
time: 30.8 us; the launch traced here: 30.6 us
  Pallas kernels  27.4 us (89%)
  local copies, waits for them, and re-layouts  2.59 us (8%)
  between operations  0.64 us (2%)
    pallas_call x1, Pallas kernels, on_device(): pl.pallas_call(functools.partial(kernel, (n_band, n_pair, points, per_own...  27.4 us
    unnamed x2, local copies, waits for them, and re-layouts  2.59 us

profile of v1, /device:TPU:0, one launch (start us, length us, event | category | flops | bytes accessed | tf_op | source)
XLA Modules:
  0.0 30.6 jit_solution(13962387433084099156)
XLA Ops:
  0.6 27.4 %shard_map.86 = (f32[2,8,1024]{2,1,0:T(8,128)}, f32[2]{0:T(128)}) custom-call(s32[8]{0:T(128)} %plan_hbm.1, f32[16]{0:T(128)} %occ_hbm.1, bf16[2,32,1024]{2,1,0:T(8,128)(2,1)} %orb_ref.1, f32[32,1024]{1,0:T(8,128)} %ker_hbm.1, f32[24,32]{1,0:T(8,128)} %constant.6.clone.cos_hbm, bf16[3,512,512]{2,1,0:T(8,128)(2,1)} %constant.7.clone.maps_hbm, ...), custom_call_target="tpu_custom_call" | custom-call | tf_op jit(solution)/shard_map/pallas_call | solution.py:322
  28.0 1.5 %copy.11 = f32[2,8,1024]{2,1,0:T(8,128)} copy(f32[2,8,1024]{2,1,0:T(8,128)} %get-tuple-element.4) | data formatting | bytes 131072
  29.5 1.1 %copy.12 = f32[2]{0:T(128)} copy(f32[2]{0:T(128)} %get-tuple-element.5) | data formatting | bytes 16

commit v2 on v1

v2 whole, which is shorter than its diff:
```python
import functools
import math

import jax
import jax.numpy as jnp
import ml_dtypes
import numpy as np
from jax import lax
from jax.experimental import pallas as pl
from jax.experimental.pallas import tpu as pltpu
from jax.sharding import PartitionSpec as P

MESH = pl.DeviceIdType.MESH
F32 = jnp.float32
BF16 = jnp.bfloat16


def pieces(value, count):
    terms = []
    for at in range(count):
        term = value.astype(BF16)
        terms.append(term)
        if at < count - 1:
            value = value - term.astype(F32)
    return terms


def tables(points, planes):
    half = points // 2
    block = half * half
    sw, row, col = (x.reshape(-1) for x in np.meshgrid(np.arange(2), np.arange(half), np.arange(half), indexing="ij"))
    target = np.arange(2 * block)
    place = np.where(sw == 0, col, points - 1 - col)
    fold = np.zeros((2, 2 * block, 2 * block), np.float32)
    fold[0, row * points + place, target] = 1.0
    fold[1, (half - 1 - row) * points + place, target] = 1.0
    select = np.zeros((2 * block, 2 * block), np.float32)
    select[row * points + col + sw, target] = 1.0
    spot = np.arange(half) + 0.5
    basis = []
    for odd in range(2):
        mode = np.arange(half) + odd
        angle = 2.0 * np.pi * mode[:, None] * spot[None, :] / points
        edge = (mode == 0) | (mode == half)
        factor = np.where(edge, math.sqrt(1.0 / half), math.sqrt(2.0 / half))
        basis.append((np.sin(angle) if odd else np.cos(angle)) * factor[:, None])
    joint = np.stack([np.kron(basis[v], basis[w]).T for v in range(2) for w in range(2)])
    high = joint.astype(ml_dtypes.bfloat16)
    low = (joint - high.astype(np.float64)).astype(ml_dtypes.bfloat16)
    out = np.arange(planes // 2)[:, None, None]
    into = np.arange(half)[None, :, None]
    wave = 2.0 * np.pi * np.arange(points)[None, None, :] / points
    near, far = np.cos(wave * (out - into)), np.cos(wave * (out + into + 1))
    cosine = np.stack([near + far, near - far]).reshape(-1, points) / (8.0 * points)
    maps = np.concatenate([fold, select[None]]).astype(ml_dtypes.bfloat16)
    return maps, np.stack([high, low]), cosine.astype(np.float32)


def kernel(
    dims,
    plan_hbm, occ_hbm, orb_ref, ker_hbm, cos_hbm, maps_hbm, joint_hbm,
    out_ref, slot_ref,
    plan_ref, occ_ref, ker_ref, cos_ref, raw, held, maps, joint, left, right, spread, lhs, spectrum, field,
    partner_part, total, energy, tile, sums, band_in, pair_in,
    load_sem, send_sem, recv_sem, band_send, band_recv, pair_send, pair_recv,
):
    n_band, n_pair, points, per_owner = dims
    meets = n_band // n_pair
    plane = points * points
    half = points // 2
    block = half * half
    planes = points // n_pair
    pairs = per_owner * per_owner * meets
    rows = points * pairs
    me = lax.axis_index("band")
    group = lax.axis_index("pair")
    base = group * planes

    wanted_loads = (
        (orb_ref, raw), (maps_hbm, maps), (ker_hbm, ker_ref), (cos_hbm, cos_ref),
        (joint_hbm, joint), (plan_hbm, plan_ref), (occ_hbm, occ_ref),
    )
    loads = [pltpu.make_async_copy(src, dst, load_sem.at[at]) for at, (src, dst) in enumerate(wanted_loads)]
    for load in loads:
        load.start()

    barrier = pltpu.get_barrier_semaphore()
    for x in range(1, n_band):
        pl.semaphore_signal(barrier, inc=1, device_id={"band": me ^ x}, device_id_type=MESH)
    for x in range(1, n_pair):
        pl.semaphore_signal(barrier, inc=1, device_id={"pair": group ^ x}, device_id_type=MESH)

    loads[0].wait()
    loads[1].wait()
    per_a = meets * per_owner
    for v in range(2):
        cut = slice(v * 2 * block, (v + 1) * 2 * block)
        own = jnp.dot(raw[...].reshape(per_owner * points, plane)[:, cut], maps[v], preferred_element_type=F32)
        held[0, 0, :, :, cut] = own.astype(BF16).reshape(per_owner, points, 2 * block)
        for a in range(per_owner):
            for o in range(per_a):
                left[:, a * per_a + o, cut] = own[a * points : (a + 1) * points]
    tile[...] = jnp.zeros_like(tile)
    pl.semaphore_wait(barrier, n_band + n_pair - 2)

    def order(step):
        first = jnp.maximum(group, 1) - 1
        return jnp.where(step == 0, 0, 1 + lax.rem(first + step - 1 + (n_pair - 1), n_pair - 1))

    mine = held.at[0, 0]

    def move(src, chunk, member, target):
        return pltpu.make_async_remote_copy(
            src_ref=src,
            dst_ref=held.at[chunk, member],
            send_sem=send_sem.at[chunk, member],
            recv_sem=recv_sem.at[chunk, member],
            device_id={"band": target},
            device_id_type=MESH,
        )

    for m in range(1, meets):
        move(mine, 0, m, me ^ m).start()

    def send_direct(step, carry):
        chunk = order(step)
        move(mine, chunk, 0, me ^ (chunk * meets)).start()
        return carry

    lax.fori_loop(1, n_pair, send_direct, 0)

    loads[2].wait()
    loads[3].wait()
    mixed = jnp.dot(cos_ref[...], ker_ref[...], precision=lax.Precision.HIGHEST, preferred_element_type=F32)
    shifted = pltpu.roll(mixed, plane - points, 1)
    for v, source in enumerate((mixed, shifted)):
        picked = 0.0
        for term in pieces(source[:, : 2 * block], 3):
            picked = picked + jnp.dot(term, maps[2], preferred_element_type=F32)
        spread[:, v * 2 * block : (v + 1) * 2 * block] = picked
    for load in loads[4:]:
        load.wait()

    sub = lax.broadcasted_iota(jnp.int32, (pairs, 128), 0)
    member = lax.rem(sub, per_a) // per_owner
    slot_row = lax.broadcasted_iota(jnp.int32, (n_band, 128), 0)
    centre = planes // 2

    def convolve(start, t):
        lanes = slice(t * 128, (t + 1) * 128)
        even, odd = [], []
        for r in range(half):
            upper = spectrum[lax.rem(start + centre + r, points), :, lanes]
            lower = spectrum[lax.rem(start + centre - 1 - r + points, points), :, lanes]
            even.append(upper + lower)
            odd.append(upper - lower)
        result = []
        for kind, values in enumerate((even, odd)):
            for q in range(centre):
                at = (kind * centre + q) * half
                value = jnp.broadcast_to(spread[at : at + 1, lanes], (pairs, 128)) * values[0]
                for r in range(1, half):
                    value = value + jnp.broadcast_to(spread[at + r : at + r + 1, lanes], (pairs, 128)) * values[r]
                result.append(value)
        return even, odd, result

    def add_energy(acc, even, odd, result):
        for q in range(centre):
            acc = acc + even[q] * result[q] + odd[q] * result[centre + q]
        return acc

    def pair_copy(x):
        return pltpu.make_async_remote_copy(
            src_ref=tile, dst_ref=pair_in.at[x], send_sem=pair_send.at[x], recv_sem=pair_recv.at[x],
            device_id={"pair": group ^ x}, device_id_type=MESH,
        )

    def band_copy(x):
        return pltpu.make_async_remote_copy(
            src_ref=sums, dst_ref=band_in.at[x], send_sem=band_send.at[x], recv_sem=band_recv.at[x],
            device_id={"band": me ^ x}, device_id_type=MESH,
        )

    extra_step = jnp.where(group == 0, n_pair - 3, jnp.where(group == n_pair - 1, 1, n_pair - 2))
    extra_block = jnp.where(
        group == 0, n_pair - 2, jnp.where(group == n_pair - 1, 0, jnp.where(group == 1, n_pair - 1, group - 1))
    )

    def step_body(step, carry):
        chunk = order(step)

        @pl.when(step == n_pair - 1)
        def _():
            for x in range(1, n_pair):
                pair_copy(x).start()

        for m in range(1, meets):
            move(mine, chunk, m, me ^ m).wait_recv()
        for o in range(per_a):
            value = held[chunk, o // per_owner, o % per_owner].astype(F32)
            for a in range(per_owner):
                right[:, a * per_a + o, :] = value

        for u in range(0, points, 2):
            density = (left[u : u + 2] * right[u : u + 2]).reshape(2 * pairs, plane)
            part = [density[:, q * block : (q + 1) * block] for q in range(4)]
            s0, d0 = part[0] + part[1], part[0] - part[1]
            s1, d1 = part[2] + part[3], part[2] - part[3]
            for q, value in enumerate((s0 + s1, d0 + d1, s0 - s1, d0 - d1)):
                high, low = pieces(value, 2)
                lhs[q, u * pairs : (u + 2) * pairs, :block] = high
                lhs[q, u * pairs : (u + 2) * pairs, block:] = low
        for q in range(4):
            high, low = lhs[q, :, :block], lhs[q, :, block:]
            modes = jnp.dot(high, joint[0, q], preferred_element_type=F32)
            modes = modes + jnp.dot(low, joint[0, q], preferred_element_type=F32)
            modes = modes + jnp.dot(high, joint[1, q], preferred_element_type=F32)
            spectrum[:, :, q * block : (q + 1) * block] = modes.reshape(points, pairs, block)

        @pl.when(step < n_pair - 1)
        def _():
            later = order(step + 1)
            move(mine, later, 0, me ^ (later * meets)).wait_recv()
            for m in range(1, meets):
                move(held.at[later, 0], later, m, me ^ m).start()

        acc = jnp.zeros((pairs, 128), F32)
        for t in range(plane // 128):
            even, odd, result = convolve(base, t)
            acc = add_energy(acc, even, odd, result)
            for q in range(centre):
                field[step, centre + q, :, t * 128 : (t + 1) * 128] = result[q] + result[centre + q]
                field[step, centre - 1 - q, :, t * 128 : (t + 1) * 128] = result[q] - result[centre + q]
        energy[...] = acc

        @pl.when(step == extra_step)
        def _():
            acc = energy[...]
            for t in range(plane // 128):
                acc = add_energy(acc, *convolve(extra_block * planes, t))
            energy[...] = acc

        occ_b = jnp.zeros((pairs, 128), F32)
        occ_a = jnp.zeros((pairs, 128), F32)
        for m in range(meets):
            partner = me ^ (chunk * meets + m)
            for b in range(per_owner):
                weight = occ_ref[partner * per_owner + b]
                occ_b = jnp.where(lax.rem(sub, per_a) == m * per_owner + b, weight, occ_b)
        for a in range(per_owner):
            occ_a = jnp.where(sub // per_a == a, occ_ref[me * per_owner + a], occ_a)

        @pl.when(step < n_pair - 1)
        def _():
            share = energy[...] * occ_a * occ_b
            for m in range(meets):
                row = jnp.sum(jnp.where(member == m, share, 0.0), axis=0, keepdims=True)
                tile[...] += jnp.where(slot_row == chunk * meets + m, row, 0.0)

        scale = jnp.concatenate([occ_b] * (plane // 128), axis=1)[None]
        partner_part[step] = right[pl.ds(base, planes)] * scale
        return carry

    lax.fori_loop(0, n_pair, step_body, 0)

    across = (((1,), (1,)), ((), ()))
    back = n_pair * planes * pairs
    for q in range(4):
        cut = slice(q * block, (q + 1) * block)
        high, low = pieces(field[:, :, :, cut].reshape(back, block), 2)
        value = lax.dot_general(high, joint[0, q], across, preferred_element_type=F32)
        value = value + lax.dot_general(low, joint[0, q], across, preferred_element_type=F32)
        value = value + lax.dot_general(high, joint[1, q], across, preferred_element_type=F32)
        spectrum[:, :, cut] = value.reshape(points, pairs, block)

    acc = tile[...]
    for x in range(1, n_pair):
        pair_copy(x).wait()
        acc = acc + pair_in[x]
    sums[...] = acc

    for j in range(planes):
        acc = [0.0] * 4
        for step in range(n_pair):
            part = [spectrum[step * planes + j, :, q * block : (q + 1) * block] for q in range(4)]
            s0, d0 = part[0] + part[1], part[0] - part[1]
            s1, d1 = part[2] + part[3], part[2] - part[3]
            for q, value in enumerate((s0 + s1, d0 + d1, s0 - s1, d0 - d1)):
                acc[q] = acc[q] + value * partner_part[step, j, :, q * block : (q + 1) * block]
        for q in range(4):
            total[j, :, q * block : (q + 1) * block] = acc[q]

    for x in range(1, n_band):
        band_copy(x).start()

    stack = []
    for a in range(per_owner):
        value = total[:, a * per_a, :]
        for o in range(1, per_a):
            value = value + total[:, a * per_a + o, :]
        stack.append(value)
    terms = pieces(jnp.concatenate(stack, axis=0), 3)
    for v in range(2):
        cut = slice(v * 2 * block, (v + 1) * 2 * block)
        result = 0.0
        for term in terms:
            result = result + lax.dot_general(term[:, cut], maps[v], across, preferred_element_type=F32)
        out_ref[:, :, cut] = -result.reshape(per_owner, planes, 2 * block)

    acc = sums[...]
    for x in range(1, n_band):
        band_copy(x).wait()
        acc = acc + band_in[x]
    for s in range(meets):
        wanted = plan_ref[group * meets + s]
        value = jnp.sum(jnp.where(slot_row == wanted, acc, 0.0))
        slot_ref[s] = -value * (1.0 / (2.0 * n_band * per_owner * points**3))

    for m in range(1, meets):
        move(mine, 0, m, me ^ m).wait_send()

    def drain(step, carry):
        chunk = order(step)
        move(mine, chunk, 0, me ^ (chunk * meets)).wait_send()
        for m in range(1, meets):
            move(held.at[chunk, 0], chunk, m, me ^ m).wait_send()
        return carry

    lax.fori_loop(1, n_pair, drain, 0)


def solution(mesh):
    n_band, n_pair = mesh.shape["band"], mesh.shape["pair"]
    meets = n_band // n_pair

    def on_device(orbitals, ker, occupations, plan):
        per_owner, points, plane = orbitals.shape
        planes = points // n_pair
        pairs = per_owner * per_owner * meets
        block = plane // 4
        maps, joint, cosine = tables(points, planes)
        vmem = pl.BlockSpec(memory_space=pltpu.VMEM)
        smem = pl.BlockSpec(memory_space=pltpu.SMEM)
        anyw = pl.BlockSpec(memory_space=pl.ANY)
        dma = pltpu.SemaphoreType.DMA
        return pl.pallas_call(
            functools.partial(kernel, (n_band, n_pair, points, per_owner)),
            out_shape=(
                jax.ShapeDtypeStruct((per_owner, planes, plane), F32),
                jax.ShapeDtypeStruct((meets,), F32),
            ),
            in_specs=[anyw] * 7,
            out_specs=(vmem, smem),
            scratch_shapes=[
                pltpu.SMEM(plan.shape, jnp.int32),
                pltpu.SMEM(occupations.shape, F32),
                pltpu.VMEM(ker.shape, F32),
                pltpu.VMEM(cosine.shape, F32),
                pltpu.VMEM(orbitals.shape, BF16),
                pltpu.VMEM((n_pair, meets, per_owner, points, plane), BF16),
                pltpu.VMEM(maps.shape, BF16),
                pltpu.VMEM(joint.shape, BF16),
                pltpu.VMEM((points, pairs, plane), F32),
                pltpu.VMEM((points, pairs, plane), F32),
                pltpu.VMEM((cosine.shape[0], plane), F32),
                pltpu.VMEM((4, points * pairs, 2 * block), BF16),
                pltpu.VMEM((points, pairs, plane), F32),
                pltpu.VMEM((n_pair, planes, pairs, plane), F32),
                pltpu.VMEM((n_pair, planes, pairs, plane), F32),
                pltpu.VMEM((planes, pairs, plane), F32),
                pltpu.VMEM((pairs, 128), F32),
                pltpu.VMEM((n_band, 128), F32),
                pltpu.VMEM((n_band, 128), F32),
                pltpu.VMEM((n_band, n_band, 128), F32),
                pltpu.VMEM((n_pair, n_band, 128), F32),
                dma((7,)),
                dma((n_pair, meets)),
                dma((n_pair, meets)),
                dma((n_band,)),
                dma((n_band,)),
                dma((n_pair,)),
                dma((n_pair,)),
            ],
            compiler_params=pltpu.CompilerParams(
                collective_id=0, has_side_effects=True, vmem_limit_bytes=67043328
            ),
        )(plan, occupations, orbitals, ker, jnp.asarray(cosine), jnp.asarray(maps), jnp.asarray(joint))

    return jax.shard_map(
        on_device,
        mesh=mesh,
        in_specs=(P("band", None, None), P(), P(), P()),
        out_specs=(P("band", "pair", None), P("pair")),
        check_vma=False,
    )
```

time: 30.8 us -> 28.1 us (0.912)
  Pallas kernels: 27.4 us -> 24.7 us
    pallas_call x1, Pallas kernels: 27.4 us -> 24.7 us  [on_device(): pl.pallas_call(functools.partial(kernel, (n_band, n_pair, points, per_own...]
where the time goes in v2:
time: 28.1 us; the launch traced here: 27.9 us
  Pallas kernels  24.7 us (88%)
  local copies, waits for them, and re-layouts  2.59 us (9%)
  between operations  0.64 us (2%)
    pallas_call x1, Pallas kernels, on_device(): pl.pallas_call(functools.partial(kernel, (n_band, n_pair, points, per_own...  24.7 us
    unnamed x2, local copies, waits for them, and re-layouts  2.59 us

profile of v2, /device:TPU:0, one launch (start us, length us, event | category | flops | bytes accessed | tf_op | source)
XLA Modules:
  0.0 27.9 jit_solution(17122734082975596542)
XLA Ops:
  0.6 24.7 %shard_map.86 = (f32[2,8,1024]{2,1,0:T(8,128)}, f32[2]{0:T(128)}) custom-call(s32[8]{0:T(128)} %plan_hbm.1, f32[16]{0:T(128)} %occ_hbm.1, bf16[2,32,1024]{2,1,0:T(8,128)(2,1)} %orb_ref.1, f32[32,1024]{1,0:T(8,128)} %ker_hbm.1, f32[128,32]{1,0:T(8,128)} %constant.6.clone.cos_hbm, bf16[3,512,512]{2,1,0:T(8,128)(2,1)} %constant.7.clone.maps_hbm, ...), custom_call_target="tpu_custom_call" | custom-call | tf_op jit(solution)/shard_map/pallas_call | solution.py:346
  25.3 1.5 %copy.11 = f32[2,8,1024]{2,1,0:T(8,128)} copy(f32[2,8,1024]{2,1,0:T(8,128)} %get-tuple-element.4) | data formatting | bytes 131072
  26.8 1.1 %copy.12 = f32[2]{0:T(128)} copy(f32[2]{0:T(128)} %get-tuple-element.5) | data formatting | bytes 16

commit v3 on v2

--- a/solution.py
+++ b/solution.py
@@ -131,13 +131,15 @@
 
     loads[2].wait()
     loads[3].wait()
-    mixed = jnp.dot(cos_ref[...], ker_ref[...], precision=lax.Precision.HIGHEST, preferred_element_type=F32)
-    shifted = pltpu.roll(mixed, plane - points, 1)
-    for v, source in enumerate((mixed, shifted)):
+    given = ker_ref[...]
+    shifted = pltpu.roll(given, plane - points, 1)
+    for v, source in enumerate((given, shifted)):
         picked = 0.0
         for term in pieces(source[:, : 2 * block], 3):
             picked = picked + jnp.dot(term, maps[2], preferred_element_type=F32)
-        spread[:, v * 2 * block : (v + 1) * 2 * block] = picked
+        spread[:, v * 2 * block : (v + 1) * 2 * block] = jnp.dot(
+            cos_ref[...], picked, precision=lax.Precision.HIGHEST, preferred_element_type=F32
+        )
     for load in loads[4:]:
         load.wait()
 
@@ -341,7 +343,7 @@
         maps, joint, cosine = tables(points, planes)
         vmem = pl.BlockSpec(memory_space=pltpu.VMEM)
         smem = pl.BlockSpec(memory_space=pltpu.SMEM)
-        anyw = pl.BlockSpec(memory_space=pl.ANY)
+        hbm = pl.BlockSpec(memory_space=pltpu.HBM)
         dma = pltpu.SemaphoreType.DMA
         return pl.pallas_call(
             functools.partial(kernel, (n_band, n_pair, points, per_owner)),
@@ -349,7 +351,7 @@
                 jax.ShapeDtypeStruct((per_owner, planes, plane), F32),
                 jax.ShapeDtypeStruct((meets,), F32),
             ),
-            in_specs=[anyw] * 7,
+            in_specs=[hbm] * 7,
             out_specs=(vmem, smem),
             scratch_shapes=[
                 pltpu.SMEM(plan.shape, jnp.int32),
@@ -382,9 +384,12 @@
                 dma((n_pair,)),
             ],
             compiler_params=pltpu.CompilerParams(
-                collective_id=0, has_side_effects=True, vmem_limit_bytes=67043328
+                collective_id=0, has_side_effects=True, vmem_limit_bytes=48 * 1024 * 1024
             ),
-        )(plan, occupations, orbitals, ker, jnp.asarray(cosine), jnp.asarray(maps), jnp.asarray(joint))
+        )(*(
+            pltpu.with_memory_space_constraint(value, pltpu.HBM)
+            for value in (plan, occupations, orbitals, ker, jnp.asarray(cosine), jnp.asarray(maps), jnp.asarray(joint))
+        ))
 
     return jax.shard_map(
         on_device,

time: 28.1 us -> 26.5 us (0.943)
  local copies, waits for them, and re-layouts: 2.59 us -> 1.14 us
    unnamed x2, local copies, waits for them, and re-layouts: 2.59 us -> 1.14 us
where the time goes in v3:
time: 26.5 us; the launch traced here: 26.3 us
  Pallas kernels  24.6 us (93%)
  local copies, waits for them, and re-layouts  1.14 us (4%)
  between operations  0.64 us (2%)
    pallas_call x1, Pallas kernels, on_device(): pl.pallas_call(functools.partial(kernel, (n_band, n_pair, points, per_own...  24.6 us
    unnamed x2, local copies, waits for them, and re-layouts  1.14 us

profile of v3, /device:TPU:0, one launch (start us, length us, event | category | flops | bytes accessed | tf_op | source)
XLA Modules:
  0.0 26.3 jit_solution(4154185781648238228)
XLA Ops:
  0.6 24.6 %shard_map.86 = (f32[2,8,1024]{2,1,0:T(8,128)S(1)}, f32[2]{0:T(128)S(1)}) custom-call(s32[8]{0:T(128)} %plan_hbm.1, f32[16]{0:T(128)} %occ_hbm.1, bf16[2,32,1024]{2,1,0:T(8,128)(2,1)} %orb_ref.1, f32[32,1024]{1,0:T(8,128)} %ker_hbm.1, f32[128,32]{1,0:T(8,128)} %constant.6.clone.cos_hbm, bf16[3,512,512]{2,1,0:T(8,128)(2,1)} %constant.7.clone.maps_hbm, ...), custom_call_target="tpu_custom_call" | custom-call | tf_op jit(solution)/shard_map/pallas_call | solution.py:348
  25.2 0.6 %copy.11 = f32[2,8,1024]{2,1,0:T(8,128)} copy(f32[2,8,1024]{2,1,0:T(8,128)S(1)} %get-tuple-element.4) | data formatting | bytes 131072
  25.8 0.5 %copy.12 = f32[2]{0:T(128)} copy(f32[2]{0:T(128)S(1)} %get-tuple-element.5) | data formatting | bytes 16

commit v4 on v3

--- a/solution.py
+++ b/solution.py
@@ -134,9 +134,10 @@
     given = ker_ref[...]
     shifted = pltpu.roll(given, plane - points, 1)
     for v, source in enumerate((given, shifted)):
-        picked = 0.0
-        for term in pieces(source[:, : 2 * block], 3):
-            picked = picked + jnp.dot(term, maps[2], preferred_element_type=F32)
+        parts = jnp.dot(
+            jnp.concatenate(pieces(source[:, : 2 * block], 3), axis=0), maps[2], preferred_element_type=F32
+        )
+        picked = parts[:points] + parts[points : 2 * points] + parts[2 * points :]
         spread[:, v * 2 * block : (v + 1) * 2 * block] = jnp.dot(
             cos_ref[...], picked, precision=lax.Precision.HIGHEST, preferred_element_type=F32
         )
@@ -301,12 +302,12 @@
         for o in range(1, per_a):
             value = value + total[:, a * per_a + o, :]
         stack.append(value)
-    terms = pieces(jnp.concatenate(stack, axis=0), 3)
+    stacked = jnp.concatenate(pieces(jnp.concatenate(stack, axis=0), 3), axis=0)
     for v in range(2):
         cut = slice(v * 2 * block, (v + 1) * 2 * block)
-        result = 0.0
-        for term in terms:
-            result = result + lax.dot_general(term[:, cut], maps[v], across, preferred_element_type=F32)
+        parts = lax.dot_general(stacked[:, cut], maps[v], across, preferred_element_type=F32)
+        height = per_owner * planes
+        result = parts[:height] + parts[height : 2 * height] + parts[2 * height :]
         out_ref[:, :, cut] = -result.reshape(per_owner, planes, 2 * block)
 
     acc = sums[...]

time: 26.5 us -> 26.5 us (level)
  no operation moved by 1% of the time
where the time goes in v4:
time: 26.5 us; the launch traced here: 26.3 us
  Pallas kernels  24.6 us (93%)
  local copies, waits for them, and re-layouts  1.14 us (4%)
  between operations  0.64 us (2%)
    pallas_call x1, Pallas kernels, on_device(): pl.pallas_call(functools.partial(kernel, (n_band, n_pair, points, per_own...  24.6 us
    unnamed x2, local copies, waits for them, and re-layouts  1.14 us

profile of v4, /device:TPU:0, one launch (start us, length us, event | category | flops | bytes accessed | tf_op | source)
XLA Modules:
  0.0 26.3 jit_solution(6913766232834797578)
XLA Ops:
  0.6 24.6 %shard_map.86 = (f32[2,8,1024]{2,1,0:T(8,128)S(1)}, f32[2]{0:T(128)S(1)}) custom-call(s32[8]{0:T(128)} %plan_hbm.1, f32[16]{0:T(128)} %occ_hbm.1, bf16[2,32,1024]{2,1,0:T(8,128)(2,1)} %orb_ref.1, f32[32,1024]{1,0:T(8,128)} %ker_hbm.1, f32[128,32]{1,0:T(8,128)} %constant.6.clone.cos_hbm, bf16[3,512,512]{2,1,0:T(8,128)(2,1)} %constant.7.clone.maps_hbm, ...), custom_call_target="tpu_custom_call" | custom-call | tf_op jit(solution)/shard_map/pallas_call | solution.py:349
  25.2 0.6 %copy.11 = f32[2,8,1024]{2,1,0:T(8,128)} copy(f32[2,8,1024]{2,1,0:T(8,128)S(1)} %get-tuple-element.4) | data formatting | bytes 131072
  25.8 0.5 %copy.12 = f32[2]{0:T(128)} copy(f32[2]{0:T(128)S(1)} %get-tuple-element.5) | data formatting | bytes 16
